TPU v7x, 512 devices: a whole 4x8x8 slice. The times are simulated.
512 devices in a mesh: row: 16 (over x, z_hi), col: 32 (over z_lo, y, core).
Axes of the slice: x: 4, y: 8, z: 8 (z_hi: 4, z_lo: 2; z = z_hi * 2 + z_lo), core: 2. Of those that a mesh axis runs over, the one named last changes fastest.
Arguments:
- bin_features: bfloat16 [4096, 512], P('row'), may hold values from -6 to 6
- w_left: bfloat16 [512, 32], replicated, may hold values from -0.25 to 0.25
- w_right: bfloat16 [512, 32], replicated, may hold values from -0.25 to 0.25
- depth_kernel: float32 [9, 32], replicated, may hold values from -2 to 2
- w_point: bfloat16 [32, 32], replicated, may hold values from -1 to 1
- w_head: bfloat16 [32, 24], replicated, may hold values from -1 to 1
- cotangent: bfloat16 [24, 4096, 4096], P(None, 'row', 'col'), may hold values from -6 to 6
Outputs:
- grad_features: bfloat16 [4096, 512], P('row')
- grad_w_left: float32 [512, 32], replicated
- grad_w_right: float32 [512, 32], replicated
- grad_kernel: float32 [9, 32], replicated
- grad_point: float32 [32, 32], replicated
- grad_head: float32 [32, 24], replicated
All inputs are finite; a program needn't handle non-finite values.
Results may differ from a plain program's by a relative error of at most 0.019.
Values may be sent and summed in bfloat16 or wider, within the bound.
No kernel may reach another device: no remote copies, remote signals or barrier semaphores. Data moves between devices by JAX's collectives and lax.ppermute only.
A program may use at most 64 MiB of HBM per device.

v0:
```python
import math
import jax
import jax.numpy as jnp
from jax import lax
from jax.sharding import PartitionSpec as P

DILATION_STEP = 4


def from_root(block, axis, source):
    block = jnp.where(lax.axis_index(axis) == source, block, jnp.zeros_like(block))
    return lax.psum(block, axis)


def extended(x, sides, width):
    for axis, dim in sides:
        count, length = (lax.axis_size(axis), x.shape[dim])
        up = [(i, (i + 1) % count) for i in range(count - 1)]
        down = [(j, i) for i, j in up]
        last = lax.slice_in_dim(x, length - width, length, axis=dim)
        first = lax.slice_in_dim(x, 0, width, axis=dim)
        before = lax.ppermute(last, axis, up)
        after = lax.ppermute(first, axis, down)
        x = jnp.concatenate([before, x, after], axis=dim)
    return x


def silu_slope(values):
    logistic = jax.nn.sigmoid(values)
    return logistic * (1.0 + values * (1.0 - logistic))


def depthwise(kernel_taps, padded, output_rows, output_columns):
    result = jnp.zeros((padded.shape[0], output_rows, output_columns), jnp.float32)
    for kernel_tap_row in range(3):
        for kernel_tap_column in range(3):
            result = result + kernel_taps[3 * kernel_tap_row + kernel_tap_column][
                :, None, None
            ] * padded[
                :,
                DILATION_STEP * kernel_tap_row : DILATION_STEP * kernel_tap_row + output_rows,
                DILATION_STEP * kernel_tap_column : DILATION_STEP * kernel_tap_column
                + output_columns,
            ].astype(
                jnp.float32
            )
    return result


def body(bin_features, w_left, w_right, depth_kernel, w_point, w_head, cotangent):
    rows_per_tile = bin_features.shape[0]
    columns_per_tile = cotangent.shape[2]
    chans = w_left.shape[1]
    row_count = lax.axis_size("row")
    col_count = lax.axis_size("col")
    panel_ratio = col_count // row_count
    contact_map_bins = rows_per_tile * row_count
    grad_scale = 1.0 / math.sqrt(contact_map_bins)
    row_index = lax.axis_index("row")
    col_index = lax.axis_index("col")
    left_panel = jnp.dot(bin_features, w_left, preferred_element_type=jnp.float32).astype(
        jnp.bfloat16
    )
    offset = col_index % panel_ratio * columns_per_tile
    own_rows = lax.dynamic_slice_in_dim(bin_features, offset, columns_per_tile, 0)
    right_own = jnp.dot(own_rows, w_right, preferred_element_type=jnp.float32).astype(jnp.bfloat16)
    right_panel = from_root(right_own, "row", col_index // panel_ratio)
    pair_matrix = (
        left_panel.astype(jnp.float32).T[:, :, None] + right_panel.astype(jnp.float32).T[:, None, :]
    ).astype(jnp.bfloat16)
    extended_pair = extended(pair_matrix, (("row", 1), ("col", 2)), DILATION_STEP)
    convolved_map = depthwise(depth_kernel, extended_pair, rows_per_tile, columns_per_tile)
    trunk_gradient = (
        grad_scale
        * jnp.einsum("ch,hij->cij", w_head, cotangent, preferred_element_type=jnp.float32)
    ).astype(jnp.bfloat16)
    grad_hidden = jnp.einsum(
        "co,oij->cij", w_point, trunk_gradient, preferred_element_type=jnp.float32
    )
    convolved_gradient = (grad_hidden * silu_slope(convolved_map)).astype(jnp.bfloat16)
    extended_gradient = extended(convolved_gradient, (("row", 1), ("col", 2)), DILATION_STEP)
    hidden_state = jax.nn.silu(convolved_map).astype(jnp.bfloat16)
    mixed_out = jnp.einsum("co,cij->oij", w_point, hidden_state, preferred_element_type=jnp.float32)
    centre_offset = extended_pair[
        :,
        DILATION_STEP : DILATION_STEP + rows_per_tile,
        DILATION_STEP : DILATION_STEP + columns_per_tile,
    ]
    trunk_matrix = (centre_offset.astype(jnp.float32) + mixed_out).astype(jnp.bfloat16)
    conv_f32 = convolved_gradient.astype(jnp.float32)
    backward_pass = jnp.zeros((chans, rows_per_tile, columns_per_tile), jnp.float32)
    kern_terms = []
    for kernel_tap_row in range(3):
        for kernel_tap_column in range(3):
            backward_pass = backward_pass + depth_kernel[3 * kernel_tap_row + kernel_tap_column][
                :, None, None
            ] * extended_gradient[
                :,
                DILATION_STEP * (2 - kernel_tap_row) : DILATION_STEP * (2 - kernel_tap_row)
                + rows_per_tile,
                DILATION_STEP * (2 - kernel_tap_column) : DILATION_STEP * (2 - kernel_tap_column)
                + columns_per_tile,
            ].astype(
                jnp.float32
            )
            shifted_window = extended_pair[
                :,
                DILATION_STEP * kernel_tap_row : DILATION_STEP * kernel_tap_row + rows_per_tile,
                DILATION_STEP * kernel_tap_column : DILATION_STEP * kernel_tap_column
                + columns_per_tile,
            ].astype(jnp.float32)
            kern_terms.append(jnp.sum(conv_f32 * shifted_window, axis=(1, 2)))
    kernel_part = jnp.stack(kern_terms)
    pair_gradient = trunk_gradient.astype(jnp.float32) + backward_pass
    left_part = jnp.sum(pair_gradient, axis=2).T
    right_part = jnp.sum(pair_gradient, axis=1).T
    point_part = jnp.einsum(
        "fsk,gsk->fg", hidden_state, trunk_gradient, preferred_element_type=jnp.float32
    )
    head_part = jnp.einsum(
        "ydq,gdq->yg", trunk_matrix, cotangent, preferred_element_type=jnp.float32
    )
    grad_left = lax.psum(left_part, "col").astype(jnp.bfloat16)
    column_total = lax.psum(right_part, "row").astype(jnp.bfloat16)
    all_panels = lax.all_gather(column_total, "col", axis=0, tiled=True)
    grad_right = lax.dynamic_slice_in_dim(all_panels, row_index * rows_per_tile, rows_per_tile, 0)
    grad_features = (
        jnp.dot(grad_left, w_left.T, preferred_element_type=jnp.float32)
        + jnp.dot(grad_right, w_right.T, preferred_element_type=jnp.float32)
    ).astype(jnp.bfloat16)
    contract = (((0,), (0,)), ((), ()))
    wleft_part = lax.dot_general(
        bin_features, grad_left, contract, preferred_element_type=jnp.float32
    )
    wright_part = lax.dot_general(
        bin_features, grad_right, contract, preferred_element_type=jnp.float32
    )
    kernel_sum, point_sum, head_sum = lax.psum((kernel_part, point_part, head_part), ("row", "col"))
    wleft_sum, wright_sum = lax.psum((wleft_part, wright_part), "row")
    return (
        grad_features,
        grad_scale * wleft_sum,
        grad_scale * wright_sum,
        grad_scale * kernel_sum,
        grad_scale * point_sum,
        grad_scale * head_sum,
    )


def solution(mesh):
    placed = (P("row", None), P(), P(), P(), P(), P(), P(None, "row", "col"))
    return jax.shard_map(
        body,
        mesh=mesh,
        in_specs=placed,
        out_specs=(P("row", None), P(), P(), P(), P(), P()),
        check_vma=False,
    )
```

profile of v0, /device:TPU:8, one launch (start us, length us, event | category | flops | bytes accessed | tf_op | source)
XLA Modules:
  0.0 674.3 jit_solution(18254187634809960480)
XLA Ops:
  7.2 0.0 copy-start
  7.2 0.0 all-reduce.4.cloned.1.call-start
  7.3 1.1 fusion.34
  8.4 50.8 %psum.56 = bf16[32,128]{1,0:T(8,128)(2,1)S(1)} all-reduce(bf16[32,128]{1,0:T(8,128)(2,1)S(1)} %fusion.34), channel_id=1, replica_groups=mesh['row'=16,'col'=32] {'row'}, use_global_device_ids=true, to_apply=%region_0.1 | all-reduce | flops 4096 | bytes 16384 | tf_op jit(solution)/shard_map/psum | solution.py:12
  59.2 1.1 fusion.29
  60.4 0.1 copy.19
  60.5 1.7 add_convert_fusion
  62.2 1.3 collective-permute-start
  63.5 1.3 collective-permute-start.1
  64.8 3.5 multiply_convert_fusion.1
  68.3 0.0 collective-permute-done
  68.3 1.9 collective-permute-done.1
  70.2 0.3 pad_maximum_fusion.2
  70.5 2.9 fusion.51
  73.5 3.6 copy.20
  77.1 3.6 copy.22
  80.8 1.9 collective-permute-start.3
  82.7 2.6 collective-permute-start.2
  85.3 3.3 collective-permute-done.2
  88.6 3.0 copy.21
  91.6 0.0 collective-permute-done.3
  91.6 3.0 copy.23
  94.7 7.2 %maximum_maximum_fusion = (bf16[32,264,132]{2,0,1:T(8,128)(2,1)S(1)}, bf16[32,264,132]{2,0,1:T(8,128)(2,1)S(1)}) fusion(bf16[32,4,128]{2,0,1:T(8,128)(2,1)S(1)} %collective-permute-done.1, bf16[32,256,128]{2,0,1:T(8,128)(2,1)} %copy-done.1, bf16[32,4,128]{2,0,1:T(8,128)(2,1)S(1)} %collective-permute-done, bf16[32,264,4]{2,0,1:T(8,128)(2,1)} %copy.21, ...), kind=kLoop, calls=%fused_computation.20 | loop fusion | flops 17842176 | bytes 6758400 | tf_op jit(solution)/shard_map/concatenate | solution.py:24
  101.9 0.0 copy-start.13
  101.9 10.2 %multiply_convert_fusion = (bf16[32,256,128]{2,0,1:T(8,128)(2,1)}, f32[32,256,128]{2,0,1:T(8,128)}) fusion(bf16[32,264,132]{2,0,1:T(8,128)(2,1)S(1)} %get-tuple-element.34, f32[32]{0:T(128)S(1)} %get-tuple-element.48, bf16[32,4,128]{2,0,1:T(8,128)(2,1)S(1)} %collective-permute-done.1, bf16[32,256,128]{2,0,1:T(8,128)(2,1)S(1)} %copy-done.2, ...), kind=kLoop, calls=%fused_computation.50 | loop fusion | flops 36700160 | bytes 21087360 | tf_op jit(solution)/shard_map/convert_element_type | solution.py:82
  112.1 3.4 fusion.30
  115.6 3.0 convolution_bitcast_fusion.2
  118.6 0.0 copy-done.3
  118.6 0.4 copy-done.7
  119.0 13.2 %fusion.23 = (f32[32]{0:T(128)S(1)}, f32[32]{0:T(128)S(1)}, f32[32]{0:T(128)S(1)}, f32[32]{0:T(128)S(1)}, f32[32]{0:T(128)S(1)}, /*index=5*/f32[32]{0:T(128)S(1)...) fusion(bf16[32,264,132]{2,0,1:T(8,128)(2,1)} %copy-done.5, ...), kind=kOutput, calls=%fused_computation.47 | convolution fusion | flops 110100192 | bytes 23186560 | tf_op jit(solution)/shard_map/co,oij->cij/dot_general | solution.py:77
  132.3 96.0 %all-reduce = (f32[9,32]{1,0:T(8,128)S(1)}, f32[32,32]{1,0:T(8,128)S(1)}, f32[32,24]{0,1:T(8,128)S(1)}) all-reduce(f32[9,32]{1,0:T(8,128)S(1)} %stack.39, f32[32,32]{1,0:T(8,128)S(1)} %convolution_bitcast_fusion.2, f32[32,24]{0,1:T(8,128)S(1)} %fusion.30), channel_id=1, replica_groups=mesh['row'=16,'col'=32] {'row','col'}, use_global_device_ids=true, to_apply=%region_16.17 | all-reduce | flops 2080 | bytes 16640 | tf_op jit(solution)/shard_map/psum | solution.py:138
  228.3 0.6 broadcast_multiply_fusion.2
  228.9 0.8 fusion.52
  229.7 2.8 collective-permute-start.4
  232.5 1.5 collective-permute-start.5
  234.0 0.6 broadcast_multiply_fusion.3
  234.6 0.0 collective-permute-done.4
  234.6 5.1 collective-permute-done.5
  239.7 1.9 pad_maximum_fusion.3
  241.5 2.9 fusion.50
  244.5 3.6 copy.24
  248.1 3.6 copy.26
  251.8 1.9 collective-permute-start.7
  253.7 3.6 collective-permute-start.6
  257.3 0.6 broadcast_multiply_fusion.4
  257.9 1.6 collective-permute-done.6
  259.5 3.0 copy.25
  262.5 0.0 collective-permute-done.7
  262.6 3.0 copy.27
  265.6 7.2 %pad_maximum_fusion.1 = (bf16[32,264,132]{2,0,1:T(8,128)(2,1)S(1)}, bf16[32,264,132]{2,0,1:T(8,128)(2,1)S(1)}) fusion(bf16[32,264,4]{2,0,1:T(8,128)(2,1)} %copy.25, bf16[32,4,128]{2,0,1:T(8,128)(2,1)S(1)} %collective-permute-done.5, bf16[32,256,128]{2,0,1:T(8,128)(2,1)} %get-tuple-element.50, bf16[32,4,128]{2,0,1:T(8,128)(2,1)S(1)} %collective-permute-done.4, ...), kind=kLoop, calls=%fused_computation.22 | loop fusion | flops 17842176 | bytes 6758400 | tf_op jit(solution)/shard_map/concatenate | solution.py:24
  272.9 0.0 copy-start.9
  272.9 0.0 copy-start.10
  272.9 0.0 copy-start.11
  272.9 7.2 %fusion.48 = (f32[32,128]{1,0:T(8,128)S(1)}, f32[32,256]{0,1:T(8,128)S(1)}) fusion(bf16[32,264,132]{2,0,1:T(8,128)(2,1)S(1)} %get-tuple-element.30, f32[32]{0:T(128)S(1)} %get-tuple-element.48, bf16[32,256,128]{2,0,1:T(8,128)(2,1)S(1)} %copy-done.6, bf16[32,4,128]{2,0,1:T(8,128)(2,1)S(1)} %collective-permute-done.4, f32[32]{0:T(128)S(1)} %get-tuple-element.49, ...), kind=kLoop, calls=%fused_computation.100 | loop fusion | flops 33542144 | bytes 16893056 | tf_op jit(solution)/shard_map/reduce_sum | solution.py:116
  280.2 102.3 %psum.57 = bf16[256,32]{1,0:T(8,128)(2,1)S(1)} all-reduce(f32[256,32]{1,0:T(8,128)S(1)} %bitcast.73), channel_id=1, replica_groups=mesh['row'=16,'col'=32] {'col'}, use_global_device_ids=true, to_apply=%region_2.3 | all-reduce | flops 8192 | bytes 49152 | tf_op jit(solution)/shard_map/psum | solution.py:123
  382.4 0.8 convolution_bitcast_fusion.1
  383.3 0.2 fusion.54
  383.5 80.7 %psum.58 = bf16[128,32]{0,1:T(8,128)(2,1)S(1)} all-reduce(f32[128,32]{0,1:T(8,128)S(1)} %bitcast.74), channel_id=1, replica_groups=mesh['row'=16,'col'=32] {'row'}, use_global_device_ids=true, to_apply=%region_4.5 | all-reduce | flops 4096 | bytes 24576 | tf_op jit(solution)/shard_map/psum | solution.py:124
  464.2 35.4 %all_gather.3 = bf16[4096,32]{0,1:T(8,128)(2,1)S(1)} all-gather(bf16[128,32]{0,1:T(8,128)(2,1)S(1)} %psum.58), channel_id=1, replica_groups=mesh['row'=16,'col'=32] {'col'}, dimensions={0}, use_global_device_ids=true | all-gather | bytes 270336 | tf_op jit(solution)/shard_map/all_gather | solution.py:125
  499.6 0.8 convolution_bitcast_fusion
  500.3 0.0 all-reduce.4.cloned.1.call-update
  500.4 1.0 fusion.28
  501.3 164.6 %all-reduce.4.cloned.1.call-done = (f32[512,32]{0,1:T(8,128)}, f32[512,32]{0,1:T(8,128)}) async-done(((f32[512,32]{0,1:T(8,128)}, f32[512,32]{0,1:T(8,128)}), (f32[512,32]{0,1:T(8,128)}, f32[512,32]{0,1:T(8,128)})) %all-reduce.4.cloned.1.call-update) | async-done | bytes 131088 | tf_op jit(solution)/shard_map/psum | solution.py:139
  665.9 1.5 broadcast_multiply_fusion
  (25 shorter events, 0.1 us)
Async XLA Ops:
  7.2 57.7 %copy-start = (bf16[24,256,128]{2,1,0:T(8,128)(2,1)S(1)}, bf16[24,256,128]{2,1,0:T(8,128)(2,1)}, u32[]{:S(2)}) copy-start(bf16[24,256,128]{2,1,0:T(8,128)(2,1)} %param.13) | copy-start | bytes 4718596
  7.2 658.8 %all-reduce.4.cloned.1.call-start = ((), (), s32[]{:S(2)}) async-start(), calls=%async_computation | async-start | bytes 262144 | tf_op jit(solution)/shard_map/psum | solution.py:139
  62.2 8.0 %copy-start.1 = (bf16[32,256,128]{2,0,1:T(8,128)(2,1)}, bf16[32,256,128]{2,0,1:T(8,128)(2,1)S(1)}, u32[]{:S(2)}) copy-start(bf16[32,256,128]{2,0,1:T(8,128)(2,1)S(1)} %add_convert_fusion) | copy-start | bytes 6291460
  62.2 6.1 collective-permute-start
  63.5 6.7 collective-permute-start.1
  73.5 11.8 %copy-start.12 = (f32[9,32]{1,0:T(8,128)S(1)}, f32[9,32]{1,0:T(8,128)}, u32[]{:S(2)}) copy-start(f32[9,32]{1,0:T(8,128)} %param.10) | copy-start | bytes 3460
  80.8 10.9 %collective-permute-start.3 = (bf16[32,264,4]{1,0,2:T(8,128)(2,1)S(1)}, bf16[32,264,4]{1,0,2:T(8,128)(2,1)S(1)}, u32[]{:S(2)}, u32[]{:S(2)}) collective-permute-start(bf16[32,264,4]{1,0,2:T(8,128)(2,1)S(1)} %copy.22), channel_id=1, source_target_pairs={{1,0},{2,1},{3,2},{4,3},{5,4},{6,5},{7,6},{8,7},{9,8},{10,9},{11,1... | collective-permute-start | bytes 202760 | tf_op jit(solution)/shard_map/ppermute | solution.py:23
  82.7 5.9 collective-permute-start.2
  94.7 7.2 %copy-start.2 = (bf16[32,256,128]{2,0,1:T(8,128)(2,1)S(1)}, bf16[32,256,128]{2,0,1:T(8,128)(2,1)}, u32[]{:S(2)}) copy-start(bf16[32,256,128]{2,0,1:T(8,128)(2,1)} %copy-done.1) | copy-start | bytes 6291460
  101.9 10.2 %copy-start.4 = (bf16[32,264,132]{2,0,1:T(8,128)(2,1)}, bf16[32,264,132]{2,0,1:T(8,128)(2,1)S(1)}, u32[]{:S(2)}) copy-start(bf16[32,264,132]{2,0,1:T(8,128)(2,1)S(1)} %get-tuple-element.33) | copy-start | bytes 6690820
  101.9 10.2 %copy-start.5 = (bf16[32,264,132]{2,0,1:T(8,128)(2,1)}, bf16[32,264,132]{2,0,1:T(8,128)(2,1)S(1)}, u32[]{:S(2)}) copy-start(bf16[32,264,132]{2,0,1:T(8,128)(2,1)S(1)} %get-tuple-element.34) | copy-start | bytes 6690820
  101.9 10.2 %copy-start.13 = (bf16[32,32]{1,0:T(8,128)(2,1)S(1)}, bf16[32,32]{1,0:T(8,128)(2,1)}, u32[]{:S(2)}) copy-start(bf16[32,32]{1,0:T(8,128)(2,1)} %param.11) | copy-start | bytes 6148
  115.5 3.1 copy-start.3
  115.5 3.5 copy-start.7
  229.7 4.9 collective-permute-start.4
  232.5 7.2 %collective-permute-start.5 = (bf16[32,4,128]{2,0,1:T(8,128)(2,1)S(1)}, bf16[32,4,128]{2,0,1:T(8,128)(2,1)S(1)}, u32[]{:S(2)}, u32[]{:S(2)}) collective-permute-start(bf16[32,4,128]{2,0,1:T(8,128)(2,1)S(1)} %get-tuple-element.38), channel_id=1, source_target_pairs={{32,0},{64,32},{96,64},{128,96},{160,128},{192,160},{224,192},{256... | collective-permute-start | bytes 98312 | tf_op jit(solution)/shard_map/ppermute | solution.py:23
  251.8 10.8 %collective-permute-start.7 = (bf16[32,264,4]{1,0,2:T(8,128)(2,1)S(1)}, bf16[32,264,4]{1,0,2:T(8,128)(2,1)S(1)}, u32[]{:S(2)}, u32[]{:S(2)}) collective-permute-start(bf16[32,264,4]{1,0,2:T(8,128)(2,1)S(1)} %copy.26), channel_id=1, source_target_pairs={{0,1},{1,2},{2,3},{3,4},{4,5},{5,6},{6,7},{7,8},{8,9},{9,10},{10,1... | collective-permute-start | bytes 202760 | tf_op jit(solution)/shard_map/ppermute | solution.py:22
  253.7 5.8 collective-permute-start.6
  265.6 7.3 %copy-start.6 = (bf16[32,256,128]{2,0,1:T(8,128)(2,1)S(1)}, bf16[32,256,128]{2,0,1:T(8,128)(2,1)}, u32[]{:S(2)}) copy-start(bf16[32,256,128]{2,0,1:T(8,128)(2,1)} %get-tuple-element.50) | copy-start | bytes 6291460
  265.6 7.3 %copy-start.8 = (bf16[32,256,128]{2,0,1:T(8,128)(2,1)S(1)}, bf16[32,256,128]{2,0,1:T(8,128)(2,1)}, u32[]{:S(2)}) copy-start(bf16[32,256,128]{2,0,1:T(8,128)(2,1)} %multiply_convert_fusion.1) | copy-start | bytes 6291460
  272.9 109.6 %copy-start.9 = (bf16[256,512]{1,0:T(8,128)(2,1)S(1)}, bf16[256,512]{1,0:T(8,128)(2,1)}, u32[]{:S(2)}) copy-start(bf16[256,512]{1,0:T(8,128)(2,1)} %param.7) | copy-start | bytes 786436
  272.9 110.4 %copy-start.10 = (bf16[512,32]{0,1:T(8,128)(2,1)S(1)}, bf16[512,32]{0,1:T(8,128)(2,1)}, u32[]{:S(2)}) copy-start(bf16[512,32]{0,1:T(8,128)(2,1)} %param.8) | copy-start | bytes 98308
  272.9 227.5 %copy-start.11 = (bf16[512,32]{0,1:T(8,128)(2,1)S(1)}, bf16[512,32]{0,1:T(8,128)(2,1)}, u32[]{:S(2)}) copy-start(bf16[512,32]{0,1:T(8,128)(2,1)} %param.9) | copy-start | bytes 98308
Sparse Core Ops, SparseCore 0:
  500.5 165.3 all-reduce.3
where the time goes:
time: 675 us; the launch traced here: 674 us
  blocking collectives  365 us (54%)
  waiting for transfers between devices  176 us (26%)
  other arithmetic  39 us (6%)
  local copies, waits for them, and re-layouts  34 us (5%)
  matrix products  28.2 us (4%)
  starting transfers between devices  17 us (3%)
  between operations  14.4 us (2%)
    psum x1, waiting for transfers between devices, body(): wleft_sum, wright_sum = lax.psum((wleft_part, wright_part), 'row')  165 us
    psum x1, blocking collectives, body(): grad_left = lax.psum(left_part, 'col').astype(jnp.bfloat16)  102 us
    psum x1, blocking collectives, body(): lax.psum((kernel_part, point_part, head_part), ('row', 'col'))  96 us
    psum x1, blocking collectives, body(): column_total = lax.psum(right_part, 'row').astype(jnp.bfloat16)  80.7 us
    psum x1, blocking collectives, from_root(): return lax.psum(block, axis)  50.8 us
    all_gather x1, blocking collectives, body(): all_panels = lax.all_gather(column_total, 'col', axis=0, tiled=True)  35.4 us
    concatenate x4, other arithmetic, extended(): x = jnp.concatenate([before, x, after], axis=dim)  16.6 us
  transfers between devices with their start and end apart: 9, of which 5 were waited for; matrix products, arithmetic and copies ran while one was open for 2% of the time, Pallas kernels for 0%

commit v1 on v0

--- a/solution.py
+++ b/solution.py
@@ -135,7 +135,9 @@
     wright_part = lax.dot_general(
         bin_features, grad_right, contract, preferred_element_type=jnp.float32
     )
-    kernel_sum, point_sum, head_sum = lax.psum((kernel_part, point_part, head_part), ("row", "col"))
+    kernel_sum, point_sum, head_sum = lax.psum(
+        lax.psum((kernel_part, point_part, head_part), "col"), "row"
+    )
     wleft_sum, wright_sum = lax.psum((wleft_part, wright_part), "row")
     return (
         grad_features,

time: 675 us -> 575 us (0.85)
  blocking collectives: 365 us -> 271 us
    psum x1 -> x0, blocking collectives: 96 us -> none  [body(): lax.psum((kernel_part, point_part, head_part), ('row', 'col'))]
  transfers between devices with their start and end apart: 9 -> 9, of which waited for: 5 -> 4; matrix products, arithmetic and copies ran while one was open for 2% -> 3% of each run, Pallas kernels for 0% -> 0%
where the time goes in v1:
time: 575 us; the launch traced here: 574 us
  blocking collectives  271 us (47%)
  waiting for transfers between devices  173 us (30%)
  other arithmetic  38.8 us (7%)
  local copies, waits for them, and re-layouts  33.6 us (6%)
  matrix products  25 us (4%)
  starting transfers between devices  18.7 us (3%)
  between operations  14.4 us (3%)
    psum x1, waiting for transfers between devices, body(): wleft_sum, wright_sum = lax.psum((wleft_part, wright_part), 'row')  166 us
    psum x1, blocking collectives, body(): grad_left = lax.psum(left_part, 'col').astype(jnp.bfloat16)  105 us
    psum x1, blocking collectives, body(): column_total = lax.psum(right_part, 'row').astype(jnp.bfloat16)  79.6 us
    psum x1, blocking collectives, from_root(): return lax.psum(block, axis)  50.8 us
    all_gather x1, blocking collectives, body(): all_panels = lax.all_gather(column_total, 'col', axis=0, tiled=True)  35.4 us
    concatenate x4, other arithmetic, extended(): x = jnp.concatenate([before, x, after], axis=dim)  16.8 us
  transfers between devices with their start and end apart: 9, of which 4 were waited for; matrix products, arithmetic and copies ran while one was open for 3% of the time, Pallas kernels for 0%

profile of v1, /device:TPU:8, one launch (start us, length us, event | category | flops | bytes accessed | tf_op | source)
XLA Modules:
  0.0 573.8 jit_solution(6220135782979123154)
XLA Ops:
  7.2 0.0 copy-start
  7.2 0.0 all-reduce.5.cloned.1.call-start
  7.3 1.1 fusion.34
  8.4 50.8 %psum.77 = bf16[32,128]{1,0:T(8,128)(2,1)S(1)} all-reduce(bf16[32,128]{1,0:T(8,128)(2,1)S(1)} %fusion.34), channel_id=1, replica_groups=mesh['row'=16,'col'=32] {'row'}, use_global_device_ids=true, to_apply=%region_0.1 | all-reduce | flops 4096 | bytes 16384 | tf_op jit(solution)/shard_map/psum | solution.py:12
  59.2 1.1 fusion.29
  60.4 0.1 copy.19
  60.5 1.7 add_convert_fusion
  62.2 1.3 collective-permute-start
  63.5 1.3 collective-permute-start.1
  64.8 3.5 multiply_convert_fusion.1
  68.3 0.0 collective-permute-done
  68.3 1.9 collective-permute-done.1
  70.2 0.0 copy-done.1
  70.2 0.3 pad_maximum_fusion.2
  70.5 2.9 fusion.51
  73.5 3.6 copy.20
  77.1 3.6 copy.22
  80.8 1.9 collective-permute-start.3
  82.7 2.6 collective-permute-start.2
  85.3 3.3 collective-permute-done.2
  88.6 3.0 copy.21
  91.6 0.0 collective-permute-done.3
  91.6 3.0 copy.23
  94.7 7.2 %maximum_maximum_fusion = (bf16[32,264,132]{2,0,1:T(8,128)(2,1)S(1)}, bf16[32,264,132]{2,0,1:T(8,128)(2,1)S(1)}) fusion(bf16[32,4,128]{2,0,1:T(8,128)(2,1)S(1)} %collective-permute-done.1, bf16[32,256,128]{2,0,1:T(8,128)(2,1)} %copy-done.1, bf16[32,4,128]{2,0,1:T(8,128)(2,1)S(1)} %collective-permute-done, bf16[32,264,4]{2,0,1:T(8,128)(2,1)} %copy.21, ...), kind=kLoop, calls=%fused_computation.20 | loop fusion | flops 17842176 | bytes 6758400 | tf_op jit(solution)/shard_map/concatenate | solution.py:24
  101.9 0.0 copy-start.9
  101.9 9.8 %multiply_convert_fusion = (bf16[32,256,128]{2,0,1:T(8,128)(2,1)}, f32[32,256,128]{2,0,1:T(8,128)}) fusion(bf16[32,264,132]{2,0,1:T(8,128)(2,1)S(1)} %get-tuple-element.39, f32[32]{0:T(128)S(1)} %get-tuple-element.53, bf16[32,4,128]{2,0,1:T(8,128)(2,1)S(1)} %collective-permute-done.1, bf16[32,256,128]{2,0,1:T(8,128)(2,1)S(1)} %copy-done.2, ...), kind=kLoop, calls=%fused_computation.50 | loop fusion | flops 36700160 | bytes 21087360 | tf_op jit(solution)/shard_map/convert_element_type | solution.py:82
  111.7 0.0 copy-done.9
  111.7 10.2 %fusion.23 = (f32[32]{0:T(128)S(1)}, f32[32]{0:T(128)S(1)}, f32[32]{0:T(128)S(1)}, f32[32]{0:T(128)S(1)}, f32[32]{0:T(128)S(1)}, /*index=5*/f32[32]{0:T(128)S(1)...) fusion(bf16[32,264,132]{2,0,1:T(8,128)(2,1)S(1)} %get-tuple-element.39, ...), kind=kOutput, calls=%fused_computation.47 | convolution fusion | flops 110100192 | bytes 23186560 | tf_op jit(solution)/shard_map/co,oij->cij/dot_general | solution.py:77
  121.9 0.8 fusion.52
  122.6 4.5 collective-permute-start.4
  127.2 1.5 collective-permute-start.5
  128.7 3.4 fusion.30
  132.2 0.0 collective-permute-done.4
  132.2 1.7 collective-permute-done.5
  133.9 1.9 pad_maximum_fusion.3
  135.8 2.9 fusion.50
  138.7 3.6 copy.24
  142.3 3.6 copy.26
  146.0 1.9 collective-permute-start.7
  147.9 3.6 collective-permute-start.6
  151.6 2.9 convolution_bitcast_fusion.2
  154.5 0.0 collective-permute-done.6
  154.5 3.0 copy.25
  157.6 0.0 collective-permute-done.7
  157.6 3.0 copy.27
  160.6 7.4 %pad_maximum_fusion.1 = (bf16[32,264,132]{2,0,1:T(8,128)(2,1)S(1)}, bf16[32,264,132]{2,0,1:T(8,128)(2,1)S(1)}) fusion(bf16[32,264,4]{2,0,1:T(8,128)(2,1)} %copy.25, bf16[32,4,128]{2,0,1:T(8,128)(2,1)S(1)} %collective-permute-done.5, bf16[32,256,128]{2,0,1:T(8,128)(2,1)} %get-tuple-element.55, bf16[32,4,128]{2,0,1:T(8,128)(2,1)S(1)} %collective-permute-done.4, ...), kind=kLoop, calls=%fused_computation.22 | loop fusion | flops 17842176 | bytes 6758400 | tf_op jit(solution)/shard_map/concatenate | solution.py:24
  168.0 0.0 copy-done.3
  168.0 0.0 copy-start.5
  168.1 0.0 copy-start.6
  168.1 0.0 copy-start.7
  168.1 7.2 %fusion.48 = (f32[32,128]{1,0:T(8,128)S(1)}, f32[32,256]{0,1:T(8,128)S(1)}) fusion(bf16[32,264,132]{2,0,1:T(8,128)(2,1)S(1)} %get-tuple-element.35, f32[32]{0:T(128)S(1)} %get-tuple-element.53, bf16[32,256,128]{2,0,1:T(8,128)(2,1)S(1)} %copy-done.3, bf16[32,4,128]{2,0,1:T(8,128)(2,1)S(1)} %collective-permute-done.4, f32[32]{0:T(128)S(1)} %get-tuple-element.54, ...), kind=kLoop, calls=%fused_computation.100 | loop fusion | flops 33542144 | bytes 16893056 | tf_op jit(solution)/shard_map/reduce_sum | solution.py:116
  175.3 104.9 %all-reduce = (bf16[256,32]{1,0:T(8,128)(2,1)S(1)}, f32[9,32]{1,0:T(8,128)S(1)}, f32[32,32]{1,0:T(8,128)S(1)}, f32[32,24]{0,1:T(8,128)S(1)}) all-reduce(f32[256,32]{1,0:T(8,128)S(1)} %bitcast.73, f32[9,32]{1,0:T(8,128)S(1)} %stack.39, f32[32,32]{1,0:T(8,128)S(1)} %convolution_bitcast_fusion.2, ...), channel_id=1, replica_groups=mesh['row'=16,'col'=32] {'col'}, use_global_device_ids=true, to_apply=%region_2.3 | all-reduce | flops 10272 | bytes 65792 | tf_op jit(solution)/shard_map/psum | solution.py:123
  280.2 0.8 convolution_bitcast_fusion.1
  281.0 0.2 fusion.54
  281.2 79.6 %all-reduce.1 = (bf16[128,32]{0,1:T(8,128)(2,1)S(1)}, f32[9,32]{1,0:T(8,128)S(1)}, f32[32,32]{1,0:T(8,128)S(1)}, f32[32,24]{0,1:T(8,128)S(1)}) all-reduce(f32[128,32]{0,1:T(8,128)S(1)} %bitcast.74, f32[9,32]{1,0:T(8,128)S(1)} %get-tuple-element.23, f32[32,32]{1,0:T(8,128)S(1)} %get-tuple-element.24, ...), channel_id=1, replica_groups=mesh['row'=16,'col'=32] {'row'}, use_global_device_ids=true, to_apply=%region_4.5 | all-reduce | flops 6176 | bytes 41216 | tf_op jit(solution)/shard_map/psum | solution.py:124
  360.8 0.6 broadcast_multiply_fusion.3
  361.4 0.6 broadcast_multiply_fusion.2
  362.0 35.4 %all_gather.3 = bf16[4096,32]{0,1:T(8,128)(2,1)S(1)} all-gather(bf16[128,32]{0,1:T(8,128)(2,1)S(1)} %get-tuple-element.26), channel_id=1, replica_groups=mesh['row'=16,'col'=32] {'col'}, dimensions={0}, use_global_device_ids=true | all-gather | bytes 270336 | tf_op jit(solution)/shard_map/all_gather | solution.py:125
  397.4 0.8 convolution_bitcast_fusion
  398.2 1.0 fusion.28
  399.2 0.0 all-reduce.5.cloned.1.call-update
  399.2 0.6 broadcast_multiply_fusion.4
  399.8 165.7 %all-reduce.5.cloned.1.call-done = (f32[512,32]{0,1:T(8,128)}, f32[512,32]{0,1:T(8,128)}) async-done(((f32[512,32]{0,1:T(8,128)}, f32[512,32]{0,1:T(8,128)}), (f32[512,32]{0,1:T(8,128)}, f32[512,32]{0,1:T(8,128)})) %all-reduce.5.cloned.1.call-update) | async-done | bytes 131088 | tf_op jit(solution)/shard_map/psum | solution.py:141
  565.4 1.5 broadcast_multiply_fusion
  (16 shorter events, 0.1 us)
Async XLA Ops:
  7.2 57.7 %copy-start = (bf16[24,256,128]{2,1,0:T(8,128)(2,1)S(1)}, bf16[24,256,128]{2,1,0:T(8,128)(2,1)}, u32[]{:S(2)}) copy-start(bf16[24,256,128]{2,1,0:T(8,128)(2,1)} %param.13) | copy-start | bytes 4718596
  7.2 558.3 %all-reduce.5.cloned.1.call-start = ((), (), s32[]{:S(2)}) async-start(), calls=%async_computation | async-start | bytes 262144 | tf_op jit(solution)/shard_map/psum | solution.py:141
  62.2 8.0 %copy-start.1 = (bf16[32,256,128]{2,0,1:T(8,128)(2,1)}, bf16[32,256,128]{2,0,1:T(8,128)(2,1)S(1)}, u32[]{:S(2)}) copy-start(bf16[32,256,128]{2,0,1:T(8,128)(2,1)S(1)} %add_convert_fusion) | copy-start | bytes 6291460
  62.2 6.1 %collective-permute-start = (bf16[32,4,128]{2,0,1:T(8,128)(2,1)S(1)}, bf16[32,4,128]{2,0,1:T(8,128)(2,1)S(1)}, u32[]{:S(2)}, u32[]{:S(2)}) collective-permute-start(bf16[32,4,128]{2,0,1:T(8,128)(2,1)S(1)} %get-tuple-element.44), channel_id=1, source_target_pairs={{0,32},{32,64},{64,96},{96,128},{128,160},{160,192},{192,224},{224... | collective-permute-start | bytes 98312 | tf_op jit(solution)/shard_map/ppermute | solution.py:22
  63.5 6.7 %collective-permute-start.1 = (bf16[32,4,128]{2,0,1:T(8,128)(2,1)S(1)}, bf16[32,4,128]{2,0,1:T(8,128)(2,1)S(1)}, u32[]{:S(2)}, u32[]{:S(2)}) collective-permute-start(bf16[32,4,128]{2,0,1:T(8,128)(2,1)S(1)} %get-tuple-element.45), channel_id=1, source_target_pairs={{32,0},{64,32},{96,64},{128,96},{160,128},{192,160},{224,192},{256... | collective-permute-start | bytes 98312 | tf_op jit(solution)/shard_map/ppermute | solution.py:23
  73.5 11.8 %copy-start.8 = (f32[9,32]{1,0:T(8,128)S(1)}, f32[9,32]{1,0:T(8,128)}, u32[]{:S(2)}) copy-start(f32[9,32]{1,0:T(8,128)} %param.10) | copy-start | bytes 3460
  80.8 10.9 %collective-permute-start.3 = (bf16[32,264,4]{1,0,2:T(8,128)(2,1)S(1)}, bf16[32,264,4]{1,0,2:T(8,128)(2,1)S(1)}, u32[]{:S(2)}, u32[]{:S(2)}) collective-permute-start(bf16[32,264,4]{1,0,2:T(8,128)(2,1)S(1)} %copy.22), channel_id=1, source_target_pairs={{1,0},{2,1},{3,2},{4,3},{5,4},{6,5},{7,6},{8,7},{9,8},{10,9},{11,1... | collective-permute-start | bytes 202760 | tf_op jit(solution)/shard_map/ppermute | solution.py:23
  82.7 5.9 %collective-permute-start.2 = (bf16[32,264,4]{1,0,2:T(8,128)(2,1)S(1)}, bf16[32,264,4]{1,0,2:T(8,128)(2,1)S(1)}, u32[]{:S(2)}, u32[]{:S(2)}) collective-permute-start(bf16[32,264,4]{1,0,2:T(8,128)(2,1)S(1)} %copy.20), channel_id=1, source_target_pairs={{0,1},{1,2},{2,3},{3,4},{4,5},{5,6},{6,7},{7,8},{8,9},{9,10},{10,1... | collective-permute-start | bytes 202760 | tf_op jit(solution)/shard_map/ppermute | solution.py:22
  94.7 7.2 %copy-start.2 = (bf16[32,256,128]{2,0,1:T(8,128)(2,1)S(1)}, bf16[32,256,128]{2,0,1:T(8,128)(2,1)}, u32[]{:S(2)}) copy-start(bf16[32,256,128]{2,0,1:T(8,128)(2,1)} %copy-done.1) | copy-start | bytes 6291460
  101.9 9.8 %copy-start.9 = (bf16[32,32]{1,0:T(8,128)(2,1)S(1)}, bf16[32,32]{1,0:T(8,128)(2,1)}, u32[]{:S(2)}) copy-start(bf16[32,32]{1,0:T(8,128)(2,1)} %param.11) | copy-start | bytes 6148
  122.6 9.5 %collective-permute-start.4 = (bf16[32,4,128]{2,0,1:T(8,128)(2,1)S(1)}, bf16[32,4,128]{2,0,1:T(8,128)(2,1)S(1)}, u32[]{:S(2)}, u32[]{:S(2)}) collective-permute-start(bf16[32,4,128]{2,0,1:T(8,128)(2,1)S(1)} %get-tuple-element.42), channel_id=1, source_target_pairs={{0,32},{32,64},{64,96},{96,128},{128,160},{160,192},{192,224},{224... | collective-permute-start | bytes 98312 | tf_op jit(solution)/shard_map/ppermute | solution.py:22
  127.2 6.7 %collective-permute-start.5 = (bf16[32,4,128]{2,0,1:T(8,128)(2,1)S(1)}, bf16[32,4,128]{2,0,1:T(8,128)(2,1)S(1)}, u32[]{:S(2)}, u32[]{:S(2)}) collective-permute-start(bf16[32,4,128]{2,0,1:T(8,128)(2,1)S(1)} %get-tuple-element.43), channel_id=1, source_target_pairs={{32,0},{64,32},{96,64},{128,96},{160,128},{192,160},{224,192},{256... | collective-permute-start | bytes 98312 | tf_op jit(solution)/shard_map/ppermute | solution.py:23
  146.0 11.6 %collective-permute-start.7 = (bf16[32,264,4]{1,0,2:T(8,128)(2,1)S(1)}, bf16[32,264,4]{1,0,2:T(8,128)(2,1)S(1)}, u32[]{:S(2)}, u32[]{:S(2)}) collective-permute-start(bf16[32,264,4]{1,0,2:T(8,128)(2,1)S(1)} %copy.26), channel_id=1, source_target_pairs={{0,1},{1,2},{2,3},{3,4},{4,5},{5,6},{6,7},{7,8},{8,9},{9,10},{10,1... | collective-permute-start | bytes 202760 | tf_op jit(solution)/shard_map/ppermute | solution.py:22
  147.9 6.6 %collective-permute-start.6 = (bf16[32,264,4]{1,0,2:T(8,128)(2,1)S(1)}, bf16[32,264,4]{1,0,2:T(8,128)(2,1)S(1)}, u32[]{:S(2)}, u32[]{:S(2)}) collective-permute-start(bf16[32,264,4]{1,0,2:T(8,128)(2,1)S(1)} %copy.24), channel_id=1, source_target_pairs={{1,0},{2,1},{3,2},{4,3},{5,4},{6,5},{7,6},{8,7},{9,8},{10,9},{11,1... | collective-permute-start | bytes 202760 | tf_op jit(solution)/shard_map/ppermute | solution.py:23
  160.6 7.4 %copy-start.3 = (bf16[32,256,128]{2,0,1:T(8,128)(2,1)S(1)}, bf16[32,256,128]{2,0,1:T(8,128)(2,1)}, u32[]{:S(2)}) copy-start(bf16[32,256,128]{2,0,1:T(8,128)(2,1)} %get-tuple-element.55) | copy-start | bytes 6291460
  160.6 7.4 %copy-start.4 = (bf16[32,256,128]{2,0,1:T(8,128)(2,1)S(1)}, bf16[32,256,128]{2,0,1:T(8,128)(2,1)}, u32[]{:S(2)}) copy-start(bf16[32,256,128]{2,0,1:T(8,128)(2,1)} %multiply_convert_fusion.1) | copy-start | bytes 6291460
  168.0 112.1 %copy-start.5 = (bf16[256,512]{1,0:T(8,128)(2,1)S(1)}, bf16[256,512]{1,0:T(8,128)(2,1)}, u32[]{:S(2)}) copy-start(bf16[256,512]{1,0:T(8,128)(2,1)} %param.7) | copy-start | bytes 786436
  168.1 112.9 %copy-start.6 = (bf16[512,32]{0,1:T(8,128)(2,1)S(1)}, bf16[512,32]{0,1:T(8,128)(2,1)}, u32[]{:S(2)}) copy-start(bf16[512,32]{0,1:T(8,128)(2,1)} %param.8) | copy-start | bytes 98308
  168.1 230.1 %copy-start.7 = (bf16[512,32]{0,1:T(8,128)(2,1)S(1)}, bf16[512,32]{0,1:T(8,128)(2,1)}, u32[]{:S(2)}) copy-start(bf16[512,32]{0,1:T(8,128)(2,1)} %param.9) | copy-start | bytes 98308
Sparse Core Ops, SparseCore 0:
  399.3 166.0 all-reduce.4
